TPU v7x, 32 devices: a whole 2x2x4 slice. The times are simulated.
32 devices in a mesh: resp: 2 (over y), item: 16 (over z, x, core).
Axes of the slice: x: 2, y: 2, z: 4, core: 2. Of those that a mesh axis runs over, the one named last changes fastest.
Arguments:
- coupling: bfloat16 [2, 4096, 2048], P('resp', 'item'), may hold values from -6 to 6
- noise: bfloat16 [2, 4096, 2048], P('resp', 'item'), may hold values from -6 to 6
- bias: float32 [16, 256], P('item', 'resp'), may hold values from -4 to 4
- responses: int32 [1024, 4096], P(None, 'item'), may hold values 0 or 1
- indices: int32 [512], replicated, may hold values from 0 to 1023
Outputs:
- new_coupling: bfloat16 [2, 4096, 2048], P('resp', 'item')
All inputs are finite; a program needn't handle non-finite values. No bound on the sum of `responses` on one device may be relied on, other than what follows from the above.
Results may differ from a plain program's by a relative error of at most 0.0035.
Values may be sent and summed in bfloat16 or wider, within the bound.
No kernel may reach another device: no remote copies, remote signals or barrier semaphores. Data moves between devices by JAX's collectives and lax.ppermute only.
A program may use at most 64 MiB of HBM per device.

v0:
```python
import math
import jax
import jax.numpy as jnp
from jax import lax
from jax.sharding import PartitionSpec as P

DRIFT = 0.01
DATA_RATIO = 900.0
NOISE_SCALE = math.sqrt(0.02)


def shards(coupling, noise, bias, responses, indices):
    couple = coupling[0]
    item_dev = couple.shape[0]
    n_resp = lax.axis_size("resp")
    n_item = lax.axis_size("item")
    sub_len = item_dev // n_resp
    inv_root = 1.0 / math.sqrt(item_dev * n_item)
    resp_idx = lax.axis_index("resp")
    item_idx = lax.axis_index("item")
    chosen = jnp.take(responses, indices, axis=0)
    spin_vals = (2 * chosen - 1).astype(jnp.bfloat16)
    summed = lax.psum_scatter(
        lax.dot_general(
            couple, spin_vals, (((0,), (1,)), ((), ())), preferred_element_type=jnp.float32
        ),
        "item",
        scatter_dimension=0,
        tiled=True,
    )
    own_start = resp_idx * sub_len
    diag_block = lax.dynamic_slice(couple, (own_start, item_idx * sub_len), (sub_len, sub_len))
    self_weight = jnp.diagonal(diag_block).astype(jnp.float32)
    spin_slice = lax.dynamic_slice_in_dim(spin_vals, own_start, sub_len, 1).T
    own_spin = spin_slice.astype(jnp.float32)
    own_answer = lax.dynamic_slice_in_dim(chosen, own_start, sub_len, 1).astype(jnp.float32).T
    fields = (summed - self_weight[:, None] * own_spin) * inv_root + bias[0][:, None]
    residual = (own_answer - jax.nn.sigmoid(fields)).astype(jnp.bfloat16)
    gathered = lax.all_gather(residual, "item", axis=0, tiled=True)
    tiles = jnp.einsum(
        "brt,kub->rktu",
        spin_vals.reshape(-1, n_resp, sub_len),
        gathered.reshape(n_item, sub_len, -1),
        preferred_element_type=jnp.float32,
    )
    flat_tiles = tiles.reshape(n_resp, n_item, sub_len * sub_len)
    moved = lax.all_to_all(
        lax.all_to_all(flat_tiles, "resp", split_axis=0, concat_axis=0, tiled=True),
        "item",
        split_axis=1,
        concat_axis=1,
        tiled=True,
    )
    own_part = tiles.transpose(0, 2, 1, 3).reshape(item_dev, n_item * sub_len)
    mirror = (
        moved.reshape(n_resp, n_item, sub_len, sub_len)
        .transpose(0, 3, 1, 2)
        .reshape(item_dev, n_item * sub_len)
    )
    row_ids = lax.broadcasted_iota(jnp.int32, (item_dev, n_item * sub_len), 0)
    col_ids = lax.broadcasted_iota(jnp.int32, (item_dev, n_item * sub_len), 1)
    on_diag = (
        (col_ids == item_idx * sub_len + row_ids - own_start)
        & (row_ids >= own_start)
        & (row_ids < own_start + sub_len)
    )
    gradient = jnp.where(on_diag, jnp.float32(0.0), own_part + mirror) * inv_root
    current = couple.astype(jnp.float32)
    updated = (
        current
        + DRIFT * (DATA_RATIO * gradient - current)
        + NOISE_SCALE * noise[0].astype(jnp.float32)
    )
    return updated.astype(jnp.bfloat16)[None]


def solution(mesh):
    return jax.shard_map(
        shards,
        mesh=mesh,
        in_specs=(
            P("resp", "item", None),
            P("resp", "item", None),
            P("item", "resp"),
            P(None, "item"),
            P(),
        ),
        out_specs=P("resp", "item", None),
        check_vma=False,
    )
```

profile of v0, /device:TPU:11, one launch (start us, length us, event | category | flops | bytes accessed | tf_op | source)
XLA Modules:
  0.0 247.9 jit_solution(4028890291314251297)
XLA Ops:
  6.5 0.8 compare_select_fusion
  7.3 0.7 compare_and_fusion
  8.0 1.6 gather_fusion
  9.6 0.9 add_convert_fusion
  10.6 2.7 %convolution_bitcast_fusion = f32[2048,512]{0,1:T(8,128)} fusion(bf16[512,256]{1,0:T(8,128)(2,1)S(1)} %get-tuple-element.5, bf16[1,256,2048]{2,1,0:T(8,128)(2,1)S(1)} %copy-done.1), kind=kOutput, calls=%fused_computation.2 | convolution fusion | flops 536870912 | bytes 5505024 | tf_op jit(solution)/shard_map/dot_general | solution.py:24
  13.2 0.0 reduce-scatter.2.cloned.1.call-update
  13.3 0.0 all-gather.2.cloned.1.call-start
  13.4 1.5 gather_fusion.1
  14.9 69.9 %reduce-scatter.2.cloned.1.call-done = f32[128,512]{0,1:T(8,128)} async-done(((f32[2048,512]{0,1:T(8,128)}), f32[128,512]{0,1:T(8,128)}) %reduce-scatter.2.cloned.1.call-update) | async-done | bytes 262160 | tf_op jit(solution)/shard_map/reduce_scatter | solution.py:23
  84.8 1.7 fusion.15
  86.5 43.1 %all-gather.2.cloned.1.call-done = bf16[2048,512]{0,1:T(8,128)(2,1)} async-done(((bf16[128,512]{0,1:T(8,128)(2,1)}), bf16[2048,512]{0,1:T(8,128)(2,1)}) %all-gather.2.cloned.1.call-update) | async-done | bytes 2097168 | tf_op jit(solution)/shard_map/all_gather | solution.py:39
  129.6 3.9 %copy.19 = bf16[2048,512]{1,0:T(8,128)(2,1)} copy(bf16[2048,512]{0,1:T(8,128)(2,1)} %all-gather.2.cloned.1.call-done) | data formatting | bytes 4194304 | tf_op jit(solution)/shard_map/reshape | solution.py:43
  133.5 2.3 fusion.6
  135.8 1.8 copy.15
  137.7 2.7 %reshape.138 = f32[2,16,16384]{2,1,0:T(8,128)} reshape(f32[2,16,128,128]{3,2,1,0:T(8,128)} %copy.15) | data formatting | bytes 4194304 | tf_op jit(solution)/shard_map/reshape | solution.py:46
  140.4 28.5 %all_to_all.10 = f32[2,16,16384]{2,1,0:T(8,128)S(1)} all-to-all(f32[2,16,16384]{2,1,0:T(8,128)} %reshape.138), channel_id=1, replica_groups=mesh['resp'=2,'item'=16] {'resp'}, dimensions={0} | all-to-all | bytes 4194304 | tf_op jit(solution)/shard_map/all_to_all | solution.py:48
  168.9 2.9 %copy.16 = f32[2,16,16384]{2,0,1:T(2,128)} copy(f32[2,16,16384]{2,1,0:T(8,128)S(1)} %all_to_all.10) | data formatting | bytes 4194304 | tf_op jit(solution)/shard_map/all_to_all | solution.py:48
  171.8 5.8 %all-to-all-start.1 = ((f32[2,16,16384]{2,0,1:T(2,128)}), f32[2,16,16384]{2,0,1:T(2,128)}, u32[]{:S(2)}, u32[]{:S(2)}) async-start(f32[2,16,16384]{2,0,1:T(2,128)} %copy.16), calls=%async_computation.2 | async-start | bytes 4194304 | tf_op jit(solution)/shard_map/all_to_all | solution.py:47
  177.7 47.5 %all-to-all-done.1 = f32[2,16,16384]{2,0,1:T(2,128)} async-done(((f32[2,16,16384]{2,0,1:T(2,128)}), f32[2,16,16384]{2,0,1:T(2,128)}, u32[]{:S(2)}, u32[]{:S(2)}) %all-to-all-start.1) | async-done | bytes 2097184 | tf_op jit(solution)/shard_map/all_to_all | solution.py:47
  225.2 4.0 %reshape.139 = f32[2,16,128,128]{3,2,0,1:T(8,128)} reshape(f32[2,16,16384]{2,0,1:T(2,128)} %all-to-all-done.1) | data formatting | bytes 4194304 | tf_op jit(solution)/shard_map/reshape | solution.py:56
  229.2 3.2 %bitcast_add_fusion = f32[2,128,16,128]{1,3,0,2:T(8,128)} fusion(f32[2,16,128,128]{3,2,0,1:T(8,128)} %reshape.139, f32[16,128,2,128]{3,1,2,0:T(8,128)S(1)} %fusion.6), kind=kLoop, calls=%fused_computation.8 | loop fusion | flops 524288 | bytes 6291456 | tf_op jit(solution)/shard_map/add | solution.py:67
  232.4 3.1 %copy.17 = f32[2,128,16,128]{3,2,1,0:T(8,128)} copy(f32[2,128,16,128]{1,3,0,2:T(8,128)} %bitcast_add_fusion) | data formatting | bytes 4194304 | tf_op jit(solution)/shard_map/add | solution.py:67
  235.5 1.7 add.87
  237.2 3.9 %fusion.2 = bf16[1,256,2048]{2,1,0:T(8,128)(2,1)} fusion(bf16[1,256,2048]{2,1,0:T(8,128)(2,1)} %param.5, bf16[1,256,2048]{2,1,0:T(8,128)(2,1)} %param.6, f32[1,256,2048]{2,1,0:T(8,128)S(1)} %add.87, s32[256]{0:T(256)S(1)} %add_subtract_fusion, pred[256]{0:T(512)(128)(4,1)S(1)} %get-tuple-element.7, pred[256]{0:T(512)(128)(4,1)S(1)} %get-tuple-element.8), kind=kLoop, calls=%fused_computation.7 | loop fusion | flops 6815744 | bytes 5244416 | tf_op jit(solution)/shard_map/convert_element_type | solution.py:74
  (16 shorter events, 0.1 us)
Async XLA Ops:
  6.5 1.5 copy-start
  6.5 78.2 %reduce-scatter.2.cloned.1.call-start = ((), (), s32[]{:S(2)}) async-start(), calls=%async_computation.3 | async-start | bytes 4456448 | tf_op jit(solution)/shard_map/reduce_scatter | solution.py:23
  8.0 2.5 %copy-start.1 = (bf16[1,256,2048]{2,1,0:T(8,128)(2,1)S(1)}, bf16[1,256,2048]{2,1,0:T(8,128)(2,1)}, u32[]{:S(2)}) copy-start(bf16[1,256,2048]{2,1,0:T(8,128)(2,1)} %param.5) | copy-start | bytes 3145732
  13.2 71.5 %copy-start.2 = (s32[512,256]{1,0:T(8,128)S(1)}, s32[512,256]{1,0:T(8,128)}, u32[]{:S(2)}) copy-start(s32[512,256]{1,0:T(8,128)} %get-tuple-element.6) | copy-start | bytes 1572868
  13.2 71.5 %copy-start.3 = (f32[1,128]{1,0:T(1,128)S(1)}, f32[1,128]{1,0:T(1,128)}, u32[]{:S(2)}) copy-start(f32[1,128]{1,0:T(1,128)} %param.7) | copy-start | bytes 1540
  13.3 116.3 %all-gather.2.cloned.1.call-start = ((), (), s32[]{:S(2)}) async-start(), calls=%async_computation.4 | async-start | bytes 2228224 | tf_op jit(solution)/shard_map/all_gather | solution.py:39
  171.8 53.4 %all-to-all-start.1 = ((f32[2,16,16384]{2,0,1:T(2,128)}), f32[2,16,16384]{2,0,1:T(2,128)}, u32[]{:S(2)}, u32[]{:S(2)}) async-start(f32[2,16,16384]{2,0,1:T(2,128)} %copy.16), calls=%async_computation.2 | async-start | bytes 4194304 | tf_op jit(solution)/shard_map/all_to_all | solution.py:47
Sparse Core Ops, SparseCore 0:
  13.4 71.3 reduce-scatter.1
  87.1 42.4 all-gather.1
where the time goes:
time: 248 us
  waiting for transfers between devices  161 us (65%)
  blocking collectives  28.5 us (11%)
  local copies, waits for them, and re-layouts  23.4 us (9%)
  between operations  13.5 us (5%)
  other arithmetic  11.2 us (5%)
  starting transfers between devices  5.89 us (2%)
  matrix products  4.96 us (2%)
    reduce_scatter x1, waiting for transfers between devices, shards(): lax.psum_scatter(lax.dot_general(couple, spin_vals, (((0,), (1,)), ((), (...  69.9 us
    all_to_all x1, waiting for transfers between devices, shards(): lax.all_to_all(lax.all_to_all(flat_tiles, 'resp', split_axis=0, concat_ax...  47.5 us
    all_gather x1, waiting for transfers between devices, shards(): gathered = lax.all_gather(residual, 'item', axis=0, tiled=True)  43.1 us
    all_to_all x1, blocking collectives, shards(): lax.all_to_all(flat_tiles, 'resp', split_axis=0, concat_axis=0, tiled=True)  28.5 us
    all_to_all x1, starting transfers between devices, shards(): lax.all_to_all(lax.all_to_all(flat_tiles, 'resp', split_axis=0, concat_ax...  5.85 us
  transfers between devices with their start and end apart: 3, of which 3 were waited for; matrix products, arithmetic and copies ran while one was open for 1% of the time, Pallas kernels for 0%

commit v1 on v0

--- a/solution.py
+++ b/solution.py
@@ -7,6 +7,19 @@
 DRIFT = 0.01
 DATA_RATIO = 900.0
 NOISE_SCALE = math.sqrt(0.02)
+
+
+def gather_around(x, axis, dim):
+    ways = lax.axis_size(axis)
+    up = [(d, (d + 1) % ways) for d in range(ways)]
+    down = [(d, (d - 1) % ways) for d in range(ways)]
+    earlier, later = ([x], [x])
+    for _ in range(ways // 2):
+        earlier.append(lax.ppermute(earlier[-1], axis, up))
+    for _ in range((ways - 1) // 2):
+        later.append(lax.ppermute(later[-1], axis, down))
+    line = jnp.concatenate([*earlier[::-1], *later[1:]], axis=dim)
+    return jnp.roll(line, (lax.axis_index(axis) - ways // 2) * x.shape[dim], axis=dim)
 
 
 def shards(coupling, noise, bias, responses, indices):
@@ -36,7 +49,7 @@
     own_answer = lax.dynamic_slice_in_dim(chosen, own_start, sub_len, 1).astype(jnp.float32).T
     fields = (summed - self_weight[:, None] * own_spin) * inv_root + bias[0][:, None]
     residual = (own_answer - jax.nn.sigmoid(fields)).astype(jnp.bfloat16)
-    gathered = lax.all_gather(residual, "item", axis=0, tiled=True)
+    gathered = gather_around(residual, "item", 0)
     tiles = jnp.einsum(
         "brt,kub->rktu",
         spin_vals.reshape(-1, n_resp, sub_len),

time: 248 us -> 259 us (1.044)
  starting transfers between devices: 5.89 us -> 42.5 us
  waiting for transfers between devices: 161 us -> 136 us
    all_gather x1 -> x0, waiting for transfers between devices: 43.1 us -> none  [shards(): gathered = lax.all_gather(residual, 'item', axis=0, tiled=True)]
    ppermute x0 -> x15, starting transfers between devices: none -> 26.9 us  [the longest x8 26.9 us: gather_around(): earlier.append(lax.ppermute(earlier[-1], axis, up))]
    ppermute x0 -> x15, waiting for transfers between devices: none -> 18.2 us  [the longest x8 15.5 us: gather_around(): earlier.append(lax.ppermute(earlier[-1], axis, up))]
    all_to_all x1, starting transfers between devices: 5.85 us -> 15.6 us  [shards(): lax.all_to_all(lax.all_to_all(flat_tiles, 'resp', split_axis=0, concat_ax...]
    reshape x1 -> x0, local copies, waits for them, and re-layouts: 3.92 us -> none  [shards(): gathered.reshape(n_item, sub_len, -1)]
    dynamic_slice x0 -> x2, local copies, waits for them, and re-layouts: none -> 2.78 us  [gather_around(): jnp.roll(line, (lax.axis_index(axis) - ways // 2) * x.shape[dim], axis=dim)]
  transfers between devices with their start and end apart: 3 -> 17, of which waited for: 3 -> 11; matrix products, arithmetic and copies ran while one was open for 1% -> 1% of each run, Pallas kernels for 0% -> 0%
where the time goes in v1:
time: 259 us
  waiting for transfers between devices  136 us (53%)
  starting transfers between devices  42.5 us (16%)
  blocking collectives  28.1 us (11%)
  local copies, waits for them, and re-layouts  23.4 us (9%)
  between operations  13.8 us (5%)
  other arithmetic  10.6 us (4%)
  matrix products  4.95 us (2%)
    reduce_scatter x1, waiting for transfers between devices, shards(): lax.psum_scatter(lax.dot_general(couple, spin_vals, (((0,), (1,)), ((), (...  70 us
    all_to_all x1, waiting for transfers between devices, shards(): lax.all_to_all(lax.all_to_all(flat_tiles, 'resp', split_axis=0, concat_ax...  47.5 us
    all_to_all x1, blocking collectives, shards(): lax.all_to_all(flat_tiles, 'resp', split_axis=0, concat_axis=0, tiled=True)  28.1 us
    ppermute x8, starting transfers between devices, gather_around(): earlier.append(lax.ppermute(earlier[-1], axis, up))  26.9 us
    all_to_all x1, starting transfers between devices, shards(): lax.all_to_all(lax.all_to_all(flat_tiles, 'resp', split_axis=0, concat_ax...  15.6 us
    ppermute x8, waiting for transfers between devices, gather_around(): earlier.append(lax.ppermute(earlier[-1], axis, up))  15.5 us
  transfers between devices with their start and end apart: 17, of which 11 were waited for; matrix products, arithmetic and copies ran while one was open for 1% of the time, Pallas kernels for 0%

profile of v1, /device:TPU:11, one launch (start us, length us, event | category | flops | bytes accessed | tf_op | source)
XLA Modules:
  0.0 259.0 jit_solution(17446484577306274996)
XLA Ops:
  10.6 2.7 %convolution_bitcast_fusion = f32[2048,512]{0,1:T(8,128)} fusion(bf16[512,256]{1,0:T(8,128)(2,1)S(1)} %get-tuple-element.5, bf16[1,256,2048]{2,1,0:T(8,128)(2,1)S(1)} %copy-done.1), kind=kOutput, calls=%fused_computation.2 | convolution fusion | flops 536870912 | bytes 5505024 | tf_op jit(solution)/shard_map/dot_general | solution.py:37
  14.9 70.0 %reduce-scatter.2.cloned.1.call-done = f32[128,512]{0,1:T(8,128)} async-done(((f32[2048,512]{0,1:T(8,128)}), f32[128,512]{0,1:T(8,128)}) %reduce-scatter.2.cloned.1.call-update) | async-done | bytes 262160 | tf_op jit(solution)/shard_map/reduce_scatter | solution.py:36
  86.0 2.9 %collective-permute-start = (bf16[128,512]{0,1:T(8,128)(2,1)S(1)}, bf16[128,512]{0,1:T(8,128)(2,1)S(1)}, u32[]{:S(2)}, u32[]{:S(2)}) collective-permute-start(bf16[128,512]{0,1:T(8,128)(2,1)S(1)} %fusion.15), channel_id=1, source_target_pairs={{0,1},{1,2},{2,3},{3,4},{4,5},{5,6},{6,7},{7,8},{8,9},{9,10},{10,1... | collective-permute-start | bytes 393224 | tf_op jit(solution)/shard_map/ppermute | solution.py:18
  88.9 1.9 collective-permute-done
  90.8 3.3 %collective-permute-start.1 = (bf16[128,512]{0,1:T(8,128)(2,1)S(1)}, bf16[128,512]{0,1:T(8,128)(2,1)S(1)}, u32[]{:S(2)}, u32[]{:S(2)}) collective-permute-start(bf16[128,512]{0,1:T(8,128)(2,1)S(1)} %collective-permute-done), channel_id=1, source_target_pairs={{0,1},{1,2},{2,3},{3,4},{4,5},{5,6},{6,7},{7,8},{8,9},{9,10},{10,1... | collective-permute-start | bytes 393224 | tf_op jit(solution)/shard_map/ppermute | solution.py:18
  94.2 1.9 collective-permute-done.1
  96.1 3.4 %collective-permute-start.2 = (bf16[128,512]{0,1:T(8,128)(2,1)S(1)}, bf16[128,512]{0,1:T(8,128)(2,1)S(1)}, u32[]{:S(2)}, u32[]{:S(2)}) collective-permute-start(bf16[128,512]{0,1:T(8,128)(2,1)S(1)} %collective-permute-done.1), channel_id=1, source_target_pairs={{0,1},{1,2},{2,3},{3,4},{4,5},{5,6},{6,7},{7,8},{8,9},{9,10},{10,1... | collective-permute-start | bytes 393224 | tf_op jit(solution)/shard_map/ppermute | solution.py:18
  101.5 3.4 %collective-permute-start.3 = (bf16[128,512]{0,1:T(8,128)(2,1)S(1)}, bf16[128,512]{0,1:T(8,128)(2,1)S(1)}, u32[]{:S(2)}, u32[]{:S(2)}) collective-permute-start(bf16[128,512]{0,1:T(8,128)(2,1)S(1)} %collective-permute-done.2), channel_id=1, source_target_pairs={{0,1},{1,2},{2,3},{3,4},{4,5},{5,6},{6,7},{7,8},{8,9},{9,10},{10,1... | collective-permute-start | bytes 393224 | tf_op jit(solution)/shard_map/ppermute | solution.py:18
  106.9 3.4 %collective-permute-start.4 = (bf16[128,512]{0,1:T(8,128)(2,1)S(1)}, bf16[128,512]{0,1:T(8,128)(2,1)S(1)}, u32[]{:S(2)}, u32[]{:S(2)}) collective-permute-start(bf16[128,512]{0,1:T(8,128)(2,1)S(1)} %collective-permute-done.3), channel_id=1, source_target_pairs={{0,1},{1,2},{2,3},{3,4},{4,5},{5,6},{6,7},{7,8},{8,9},{9,10},{10,1... | collective-permute-start | bytes 393224 | tf_op jit(solution)/shard_map/ppermute | solution.py:18
  112.3 3.4 %collective-permute-start.5 = (bf16[128,512]{0,1:T(8,128)(2,1)S(1)}, bf16[128,512]{0,1:T(8,128)(2,1)S(1)}, u32[]{:S(2)}, u32[]{:S(2)}) collective-permute-start(bf16[128,512]{0,1:T(8,128)(2,1)S(1)} %collective-permute-done.4), channel_id=1, source_target_pairs={{0,1},{1,2},{2,3},{3,4},{4,5},{5,6},{6,7},{7,8},{8,9},{9,10},{10,1... | collective-permute-start | bytes 393224 | tf_op jit(solution)/shard_map/ppermute | solution.py:18
  117.7 3.4 %collective-permute-start.6 = (bf16[128,512]{0,1:T(8,128)(2,1)S(1)}, bf16[128,512]{0,1:T(8,128)(2,1)S(1)}, u32[]{:S(2)}, u32[]{:S(2)}) collective-permute-start(bf16[128,512]{0,1:T(8,128)(2,1)S(1)} %collective-permute-done.5), channel_id=1, source_target_pairs={{0,1},{1,2},{2,3},{3,4},{4,5},{5,6},{6,7},{7,8},{8,9},{9,10},{10,1... | collective-permute-start | bytes 393224 | tf_op jit(solution)/shard_map/ppermute | solution.py:18
  123.1 3.4 %collective-permute-start.7 = (bf16[128,512]{0,1:T(8,128)(2,1)S(1)}, bf16[128,512]{0,1:T(8,128)(2,1)S(1)}, u32[]{:S(2)}, u32[]{:S(2)}) collective-permute-start(bf16[128,512]{0,1:T(8,128)(2,1)S(1)} %collective-permute-done.6), channel_id=1, source_target_pairs={{0,1},{1,2},{2,3},{3,4},{4,5},{5,6},{6,7},{7,8},{8,9},{9,10},{10,1... | collective-permute-start | bytes 393224 | tf_op jit(solution)/shard_map/ppermute | solution.py:18
  129.2 2.7 %collective-permute-done.14 = bf16[128,512]{0,1:T(8,128)(2,1)S(1)} collective-permute-done((bf16[128,512]{0,1:T(8,128)(2,1)S(1)}, bf16[128,512]{0,1:T(8,128)(2,1)S(1)}, u32[]{:S(2)}, u32[]{:S(2)}) %collective-permute-start.14) | collective-permute-done | bytes 131104 | tf_op jit(solution)/shard_map/ppermute | solution.py:20
  132.9 2.5 copy.12
  135.4 2.3 fusion.6
  139.6 2.7 %reshape.138 = f32[2,16,16384]{2,1,0:T(8,128)} reshape(f32[2,16,128,128]{3,2,1,0:T(8,128)} %copy.14) | data formatting | bytes 4194304 | tf_op jit(solution)/shard_map/reshape | solution.py:59
  142.3 28.1 %all_to_all.10 = f32[2,16,16384]{2,1,0:T(8,128)S(1)} all-to-all(f32[2,16,16384]{2,1,0:T(8,128)} %reshape.138), channel_id=1, replica_groups=mesh['resp'=2,'item'=16] {'resp'}, dimensions={0} | all-to-all | bytes 4194304 | tf_op jit(solution)/shard_map/all_to_all | solution.py:61
  170.3 2.9 %copy.15 = f32[2,16,16384]{2,0,1:T(2,128)} copy(f32[2,16,16384]{2,1,0:T(8,128)S(1)} %all_to_all.10) | data formatting | bytes 4194304 | tf_op jit(solution)/shard_map/all_to_all | solution.py:61
  173.3 15.6 %all-to-all-start.1 = ((f32[2,16,16384]{2,0,1:T(2,128)}), f32[2,16,16384]{2,0,1:T(2,128)}, u32[]{:S(2)}, u32[]{:S(2)}) async-start(f32[2,16,16384]{2,0,1:T(2,128)} %copy.15), calls=%async_computation.2 | async-start | bytes 4194304 | tf_op jit(solution)/shard_map/all_to_all | solution.py:60
  188.9 47.5 %all-to-all-done.1 = f32[2,16,16384]{2,0,1:T(2,128)} async-done(((f32[2,16,16384]{2,0,1:T(2,128)}), f32[2,16,16384]{2,0,1:T(2,128)}, u32[]{:S(2)}, u32[]{:S(2)}) %all-to-all-start.1) | async-done | bytes 2097184 | tf_op jit(solution)/shard_map/all_to_all | solution.py:60
  236.4 4.0 %reshape.139 = f32[2,16,128,128]{3,2,0,1:T(8,128)} reshape(f32[2,16,16384]{2,0,1:T(2,128)} %all-to-all-done.1) | data formatting | bytes 4194304 | tf_op jit(solution)/shard_map/reshape | solution.py:69
  240.4 3.1 %bitcast_add_fusion = f32[2,128,16,128]{1,3,0,2:T(8,128)} fusion(f32[2,16,128,128]{3,2,0,1:T(8,128)} %reshape.139, f32[16,128,2,128]{3,1,2,0:T(8,128)S(1)} %fusion.6), kind=kLoop, calls=%fused_computation.8 | loop fusion | flops 524288 | bytes 6291456 | tf_op jit(solution)/shard_map/add | solution.py:80
  243.5 3.0 %copy.16 = f32[2,128,16,128]{3,2,1,0:T(8,128)} copy(f32[2,128,16,128]{1,3,0,2:T(8,128)} %bitcast_add_fusion) | data formatting | bytes 4194304 | tf_op jit(solution)/shard_map/add | solution.py:80
  248.3 3.9 %fusion.2 = bf16[1,256,2048]{2,1,0:T(8,128)(2,1)} fusion(bf16[1,256,2048]{2,1,0:T(8,128)(2,1)} %param.5, bf16[1,256,2048]{2,1,0:T(8,128)(2,1)} %param.6, f32[1,256,2048]{2,1,0:T(8,128)S(1)} %add.100, s32[256]{0:T(256)S(1)} %add_subtract_fusion, pred[256]{0:T(512)(128)(4,1)S(1)} %iota_compare_fusion.1, pred[256]{0:T(512)(128)(4,1)S(1)} %iota_compare_fusion.2), kind=kLoop, calls=%fused_computation.7 | loop fusion | flops 6815744 | bytes 5244416 | tf_op jit(solution)/shard_map/convert_element_type | solution.py:87
  (77 shorter events, 23.4 us)
Async XLA Ops:
  6.5 1.5 copy-start
  6.5 4.1 %copy-start.1 = (bf16[1,256,2048]{2,1,0:T(8,128)(2,1)S(1)}, bf16[1,256,2048]{2,1,0:T(8,128)(2,1)}, u32[]{:S(2)}) copy-start(bf16[1,256,2048]{2,1,0:T(8,128)(2,1)} %param.5) | copy-start | bytes 3145732
  6.5 78.4 %reduce-scatter.2.cloned.1.call-start = ((), (), s32[]{:S(2)}) async-start(), calls=%async_computation.3 | async-start | bytes 4456448 | tf_op jit(solution)/shard_map/reduce_scatter | solution.py:36
  13.3 71.6 %copy-start.2 = (s32[512,256]{1,0:T(8,128)S(1)}, s32[512,256]{1,0:T(8,128)}, u32[]{:S(2)}) copy-start(s32[512,256]{1,0:T(8,128)} %get-tuple-element.6) | copy-start | bytes 1572868
  13.3 71.6 %copy-start.3 = (f32[1,128]{1,0:T(1,128)S(1)}, f32[1,128]{1,0:T(1,128)}, u32[]{:S(2)}) copy-start(f32[1,128]{1,0:T(1,128)} %param.7) | copy-start | bytes 1540
  86.0 4.8 %collective-permute-start = (bf16[128,512]{0,1:T(8,128)(2,1)S(1)}, bf16[128,512]{0,1:T(8,128)(2,1)S(1)}, u32[]{:S(2)}, u32[]{:S(2)}) collective-permute-start(bf16[128,512]{0,1:T(8,128)(2,1)S(1)} %fusion.15), channel_id=1, source_target_pairs={{0,1},{1,2},{2,3},{3,4},{4,5},{5,6},{6,7},{7,8},{8,9},{9,10},{10,1... | collective-permute-start | bytes 393224 | tf_op jit(solution)/shard_map/ppermute | solution.py:18
  90.8 5.3 %collective-permute-start.1 = (bf16[128,512]{0,1:T(8,128)(2,1)S(1)}, bf16[128,512]{0,1:T(8,128)(2,1)S(1)}, u32[]{:S(2)}, u32[]{:S(2)}) collective-permute-start(bf16[128,512]{0,1:T(8,128)(2,1)S(1)} %collective-permute-done), channel_id=1, source_target_pairs={{0,1},{1,2},{2,3},{3,4},{4,5},{5,6},{6,7},{7,8},{8,9},{9,10},{10,1... | collective-permute-start | bytes 393224 | tf_op jit(solution)/shard_map/ppermute | solution.py:18
  94.2 5.4 %collective-permute-start.8 = (bf16[128,512]{0,1:T(8,128)(2,1)S(1)}, bf16[128,512]{0,1:T(8,128)(2,1)S(1)}, u32[]{:S(2)}, u32[]{:S(2)}) collective-permute-start(bf16[128,512]{0,1:T(8,128)(2,1)S(1)} %fusion.15), channel_id=1, source_target_pairs={{0,15},{1,0},{2,1},{3,2},{4,3},{5,4},{6,5},{7,6},{8,7},{9,8},{10,9... | collective-permute-start | bytes 393224 | tf_op jit(solution)/shard_map/ppermute | solution.py:20
  96.1 5.4 %collective-permute-start.2 = (bf16[128,512]{0,1:T(8,128)(2,1)S(1)}, bf16[128,512]{0,1:T(8,128)(2,1)S(1)}, u32[]{:S(2)}, u32[]{:S(2)}) collective-permute-start(bf16[128,512]{0,1:T(8,128)(2,1)S(1)} %collective-permute-done.1), channel_id=1, source_target_pairs={{0,1},{1,2},{2,3},{3,4},{4,5},{5,6},{6,7},{7,8},{8,9},{9,10},{10,1... | collective-permute-start | bytes 393224 | tf_op jit(solution)/shard_map/ppermute | solution.py:18
  99.6 5.4 %collective-permute-start.9 = (bf16[128,512]{0,1:T(8,128)(2,1)S(1)}, bf16[128,512]{0,1:T(8,128)(2,1)S(1)}, u32[]{:S(2)}, u32[]{:S(2)}) collective-permute-start(bf16[128,512]{0,1:T(8,128)(2,1)S(1)} %collective-permute-done.8), channel_id=1, source_target_pairs={{0,15},{1,0},{2,1},{3,2},{4,3},{5,4},{6,5},{7,6},{8,7},{9,8},{10,9... | collective-permute-start | bytes 393224 | tf_op jit(solution)/shard_map/ppermute | solution.py:20
  101.5 5.4 %collective-permute-start.3 = (bf16[128,512]{0,1:T(8,128)(2,1)S(1)}, bf16[128,512]{0,1:T(8,128)(2,1)S(1)}, u32[]{:S(2)}, u32[]{:S(2)}) collective-permute-start(bf16[128,512]{0,1:T(8,128)(2,1)S(1)} %collective-permute-done.2), channel_id=1, source_target_pairs={{0,1},{1,2},{2,3},{3,4},{4,5},{5,6},{6,7},{7,8},{8,9},{9,10},{10,1... | collective-permute-start | bytes 393224 | tf_op jit(solution)/shard_map/ppermute | solution.py:18
  105.0 5.4 %collective-permute-start.10 = (bf16[128,512]{0,1:T(8,128)(2,1)S(1)}, bf16[128,512]{0,1:T(8,128)(2,1)S(1)}, u32[]{:S(2)}, u32[]{:S(2)}) collective-permute-start(bf16[128,512]{0,1:T(8,128)(2,1)S(1)} %collective-permute-done.9), channel_id=1, source_target_pairs={{0,15},{1,0},{2,1},{3,2},{4,3},{5,4},{6,5},{7,6},{8,7},{9,8},{10,9... | collective-permute-start | bytes 393224 | tf_op jit(solution)/shard_map/ppermute | solution.py:20
  106.9 5.4 %collective-permute-start.4 = (bf16[128,512]{0,1:T(8,128)(2,1)S(1)}, bf16[128,512]{0,1:T(8,128)(2,1)S(1)}, u32[]{:S(2)}, u32[]{:S(2)}) collective-permute-start(bf16[128,512]{0,1:T(8,128)(2,1)S(1)} %collective-permute-done.3), channel_id=1, source_target_pairs={{0,1},{1,2},{2,3},{3,4},{4,5},{5,6},{6,7},{7,8},{8,9},{9,10},{10,1... | collective-permute-start | bytes 393224 | tf_op jit(solution)/shard_map/ppermute | solution.py:18
  110.3 5.4 %collective-permute-start.11 = (bf16[128,512]{0,1:T(8,128)(2,1)S(1)}, bf16[128,512]{0,1:T(8,128)(2,1)S(1)}, u32[]{:S(2)}, u32[]{:S(2)}) collective-permute-start(bf16[128,512]{0,1:T(8,128)(2,1)S(1)} %collective-permute-done.10), channel_id=1, source_target_pairs={{0,15},{1,0},{2,1},{3,2},{4,3},{5,4},{6,5},{7,6},{8,7},{9,8},{10,9... | collective-permute-start | bytes 393224 | tf_op jit(solution)/shard_map/ppermute | solution.py:20
  112.3 5.4 %collective-permute-start.5 = (bf16[128,512]{0,1:T(8,128)(2,1)S(1)}, bf16[128,512]{0,1:T(8,128)(2,1)S(1)}, u32[]{:S(2)}, u32[]{:S(2)}) collective-permute-start(bf16[128,512]{0,1:T(8,128)(2,1)S(1)} %collective-permute-done.4), channel_id=1, source_target_pairs={{0,1},{1,2},{2,3},{3,4},{4,5},{5,6},{6,7},{7,8},{8,9},{9,10},{10,1... | collective-permute-start | bytes 393224 | tf_op jit(solution)/shard_map/ppermute | solution.py:18
  115.7 5.4 %collective-permute-start.12 = (bf16[128,512]{0,1:T(8,128)(2,1)S(1)}, bf16[128,512]{0,1:T(8,128)(2,1)S(1)}, u32[]{:S(2)}, u32[]{:S(2)}) collective-permute-start(bf16[128,512]{0,1:T(8,128)(2,1)S(1)} %collective-permute-done.11), channel_id=1, source_target_pairs={{0,15},{1,0},{2,1},{3,2},{4,3},{5,4},{6,5},{7,6},{8,7},{9,8},{10,9... | collective-permute-start | bytes 393224 | tf_op jit(solution)/shard_map/ppermute | solution.py:20
  117.7 5.4 %collective-permute-start.6 = (bf16[128,512]{0,1:T(8,128)(2,1)S(1)}, bf16[128,512]{0,1:T(8,128)(2,1)S(1)}, u32[]{:S(2)}, u32[]{:S(2)}) collective-permute-start(bf16[128,512]{0,1:T(8,128)(2,1)S(1)} %collective-permute-done.5), channel_id=1, source_target_pairs={{0,1},{1,2},{2,3},{3,4},{4,5},{5,6},{6,7},{7,8},{8,9},{9,10},{10,1... | collective-permute-start | bytes 393224 | tf_op jit(solution)/shard_map/ppermute | solution.py:18
  121.1 5.4 %collective-permute-start.13 = (bf16[128,512]{0,1:T(8,128)(2,1)S(1)}, bf16[128,512]{0,1:T(8,128)(2,1)S(1)}, u32[]{:S(2)}, u32[]{:S(2)}) collective-permute-start(bf16[128,512]{0,1:T(8,128)(2,1)S(1)} %collective-permute-done.12), channel_id=1, source_target_pairs={{0,15},{1,0},{2,1},{3,2},{4,3},{5,4},{6,5},{7,6},{8,7},{9,8},{10,9... | collective-permute-start | bytes 393224 | tf_op jit(solution)/shard_map/ppermute | solution.py:20
  123.1 5.4 %collective-permute-start.7 = (bf16[128,512]{0,1:T(8,128)(2,1)S(1)}, bf16[128,512]{0,1:T(8,128)(2,1)S(1)}, u32[]{:S(2)}, u32[]{:S(2)}) collective-permute-start(bf16[128,512]{0,1:T(8,128)(2,1)S(1)} %collective-permute-done.6), channel_id=1, source_target_pairs={{0,1},{1,2},{2,3},{3,4},{4,5},{5,6},{6,7},{7,8},{8,9},{9,10},{10,1... | collective-permute-start | bytes 393224 | tf_op jit(solution)/shard_map/ppermute | solution.py:18
  126.5 5.3 %collective-permute-start.14 = (bf16[128,512]{0,1:T(8,128)(2,1)S(1)}, bf16[128,512]{0,1:T(8,128)(2,1)S(1)}, u32[]{:S(2)}, u32[]{:S(2)}) collective-permute-start(bf16[128,512]{0,1:T(8,128)(2,1)S(1)} %collective-permute-done.13), channel_id=1, source_target_pairs={{0,15},{1,0},{2,1},{3,2},{4,3},{5,4},{6,5},{7,6},{8,7},{9,8},{10,9... | collective-permute-start | bytes 393224 | tf_op jit(solution)/shard_map/ppermute | solution.py:20
  173.3 63.1 %all-to-all-start.1 = ((f32[2,16,16384]{2,0,1:T(2,128)}), f32[2,16,16384]{2,0,1:T(2,128)}, u32[]{:S(2)}, u32[]{:S(2)}) async-start(f32[2,16,16384]{2,0,1:T(2,128)} %copy.15), calls=%async_computation.2 | async-start | bytes 4194304 | tf_op jit(solution)/shard_map/all_to_all | solution.py:60
Sparse Core Ops, SparseCore 0:
  13.4 71.4 reduce-scatter.1
